TPU v7x, 256 devices: a whole 4x4x8 slice. The times are simulated.
256 devices in a mesh: rows: 64 (over x, z, core), cols: 4 (over y).
Axes of the slice: x: 4, y: 4, z: 8, core: 2. Of those that a mesh axis runs over, the one named last changes fastest.
Arguments:
- slot_tile: int32 [64, 3], replicated, may hold values from 0 to 128, as said below
- slot_ranks: int32 [64, 3, 4], P('rows', None, 'cols'), may hold values from 0 to 256, as said below
- diag_ranks: int32 [4], P('cols'), may hold values from 32 to 256
- panel_left_factors: bfloat16 [4, 192, 1024, 256], P('cols', 'rows'), may hold values from -12 to 12
- panel_v: bfloat16 [4, 192, 1024, 256], P('cols', 'rows'), may hold values from -0.1875 to 0.1875
- diag_u: bfloat16 [4, 1024, 256], P('cols'), may hold values from -0.38 to 0.38, as said below
- diag_v: bfloat16 [4, 1024, 256], P('cols'), may hold values from -1 to 1
- panel_points: int32 [192, 2, 1024], P('rows', None, 'cols'), may hold values from 0 to 1023, as said below
- diag_points: int32 [2, 1024], replicated, may hold values from 0 to 1023, as said below
- rhs_diag: float32 [1024, 512], P(None, 'cols'), may hold values from -0.3 to 0.3
- rhs_rest: float32 [128, 4, 4, 64, 512], P(None, 'cols', None, 'rows'), may hold values from -6 to 6
Outputs:
- panel_factor: bfloat16 [192, 1024, 1024], P('rows', 'cols')
- diag_solution: float32 [1024, 512], P(None, 'cols')
- rhs_out: float32 [128, 4, 4, 64, 512], P(None, 'cols', None, 'rows')
Inputs may be any that keep to these rules, and one draw needn't show every extreme that they name: `slot_tile`: every tile 0 to 127 stands in exactly one slot; 128 marks an empty slot; the live slots of an owner come first; every owner has 1 to 3 live slots and some owner has 3. Owners are chosen by the tiles' summed ranks. `slot_ranks`: live slots have ranks 32 to 256, empty slots 0; both 32 and 256 occur. The columns of each diag_u[j] are orthogonal, with lengths 0.1 to 0.38. `panel_points`: row 0 holds x, row 1 holds y. A live slot holds the cells of a block of 32 x (32) grid cells in some order; blocks of different tiles and of the diagonal tile are distinct; an empty slot holds the points of some tile. `diag_points`: row 0 holds x, row 1 holds y: the cells of one block of 32 x (32) grid cells in some order.
All inputs are finite; a program needn't handle non-finite values.
Results may differ from a plain program's by a relative error of at most 0.0057.
Values may be sent and summed in bfloat16 or wider, within the bound.
A program may use at most 128 MiB of HBM per device.

v0:
```python
import jax
import jax.numpy as jnp
from jax import lax
from jax.sharding import PartitionSpec as P

GX = 1024
length_scale = 0.3
nugget = 1.0


def matern(first_x, first_y, second_x, second_y):
    spacing = 1.0 / GX
    delta_x = (first_x - second_x) * spacing
    delta_y = (first_y - second_y) * spacing
    scaled = jnp.sqrt(3.0) * jnp.sqrt(delta_x * delta_x + delta_y * delta_y) / length_scale
    return (1.0 + scaled) * jnp.exp(-scaled)


def owner_rows(slot_tile, tile_count, per_peer, row_devices):
    flat_tiles = slot_tile.reshape(-1)
    slot_count = flat_tiles.shape[0]
    tmax_local = slot_tile.shape[1]
    owner_slot = (
        jnp.zeros((tile_count + 1,), jnp.int32)
        .at[flat_tiles]
        .set(jnp.arange(slot_count, dtype=jnp.int32))[:tile_count]
    )
    source_row = owner_slot // tmax_local
    source_place = owner_slot % tmax_local
    step_index = jnp.arange(per_peer, dtype=jnp.int32)
    return (
        (source_place[:, None] * per_peer + step_index[None, :]) * row_devices + source_row[:, None]
    ).reshape(-1)


def times_block(owned_rows, forward):
    return jnp.dot(
        owned_rows,
        lax.all_gather(forward, "cols", axis=1, tiled=True),
        preferred_element_type=jnp.float32,
    )


def per_device(
    slot_tile,
    slot_ranks,
    diag_ranks,
    panel_left_factors,
    panel_v,
    diag_u,
    diag_v,
    panel_points,
    diag_points,
    rhs_diag,
    rhs_rest,
):
    row_devices = lax.axis_size("rows")
    col_devices = lax.axis_size("cols")
    slot_count = panel_left_factors.shape[1]
    tile_order = diag_u.shape[1]
    rank_max = diag_u.shape[2]
    quarter = tile_order // col_devices
    per_peer = quarter // row_devices
    tile_count = rhs_rest.shape[0]
    row_index = lax.axis_index("rows")
    rank_index = jnp.arange(rank_max, dtype=jnp.int32)
    diag_mask = (rank_index < diag_ranks[0]).astype(jnp.bfloat16)
    diagonal_left_factor = diag_u[0] * diag_mask[None, :]
    diagonal_right_factor = diag_v[0] * diag_mask[None, :]
    slot_mask = (rank_index[None, :] < slot_ranks[0, :, 0][:, None]).astype(jnp.bfloat16)
    slot_left_factor = panel_left_factors[0] * slot_mask[:, None, :]
    slot_right_factor = panel_v[0] * slot_mask[:, None, :]
    inner_product_core = jnp.einsum(
        "gok,oe->gke", slot_right_factor, diagonal_right_factor, preferred_element_type=jnp.float32
    ).astype(jnp.bfloat16)
    low_rows = jnp.einsum(
        "lgc,lcz->lgz", slot_left_factor, inner_product_core, preferred_element_type=jnp.float32
    ).astype(jnp.bfloat16)
    diag_core = jnp.einsum(
        "br,bq->rq",
        diagonal_right_factor,
        diagonal_right_factor,
        preferred_element_type=jnp.float32,
    ).astype(jnp.bfloat16)
    diag_low = jnp.dot(diagonal_left_factor, diag_core, preferred_element_type=jnp.float32).astype(
        jnp.bfloat16
    )
    gathered_low, gathered_left = (
        lax.all_gather(diag_low[None], "cols", axis=0, tiled=True),
        lax.all_gather(diagonal_left_factor[None], "cols", axis=0, tiled=True),
    )
    outgoing_low = low_rows.reshape(slot_count, col_devices, quarter, rank_max)
    update_term = jnp.einsum(
        "sjnr,jbr->snb",
        lax.all_to_all(outgoing_low, "cols", split_axis=1, concat_axis=1, tiled=True),
        gathered_left,
        preferred_element_type=jnp.float32,
    )
    centre = diag_points.astype(jnp.float32)
    identity = jnp.eye(tile_order, dtype=jnp.float32)
    diag_term = jnp.einsum(
        "jbr,jcr->bc", gathered_low, gathered_left, preferred_element_type=jnp.float32
    )
    own_block = matern(centre[0][:, None], centre[1][:, None], centre[0], centre[1])
    diag_system = own_block + nugget * identity - diag_term
    factor = jnp.linalg.cholesky(diag_system)
    inverse = jax.scipy.linalg.solve_triangular(factor, identity, lower=True)
    my_tiles = lax.dynamic_slice_in_dim(slot_tile, row_index, 1, 0)[0]
    live_mask = (my_tiles < tile_count).astype(jnp.float32)
    coords = panel_points.astype(jnp.float32)
    generated = matern(coords[:, 0, :, None], coords[:, 1, :, None], centre[0], centre[1])
    system_rows = live_mask[:, None, None] * (generated - update_term)
    panel_factor = jnp.einsum(
        "snb,cb->snc", system_rows, inverse, precision=lax.Precision.HIGHEST
    ).astype(jnp.bfloat16)
    diag_solution = jnp.dot(inverse, rhs_diag, precision=lax.Precision.HIGHEST)
    forward = diag_solution.astype(jnp.bfloat16)
    pick_rows = owner_rows(slot_tile, tile_count, per_peer, row_devices)
    outgoing_rows = panel_factor.reshape(slot_count, per_peer, row_devices, tile_order)
    incoming = lax.all_to_all(outgoing_rows, "rows", split_axis=2, concat_axis=2, tiled=True)
    owned_rows = jnp.take(incoming.reshape(-1, tile_order), pick_rows, axis=0)
    product = times_block(owned_rows, forward).astype(jnp.bfloat16)
    rhs_out = rhs_rest - product.reshape(rhs_rest.shape).astype(jnp.float32)
    return (panel_factor, diag_solution, rhs_out)


def solution(mesh):
    return jax.shard_map(
        per_device,
        mesh=mesh,
        in_specs=(
            P(),
            P("rows", None, "cols"),
            P("cols"),
            P("cols", "rows", None, None),
            P("cols", "rows", None, None),
            P("cols", None, None),
            P("cols", None, None),
            P("rows", None, "cols"),
            P(),
            P(None, "cols"),
            P(None, "cols", None, "rows", None),
        ),
        out_specs=(P("rows", "cols", None), P(None, "cols"), P(None, "cols", None, "rows", None)),
        check_vma=False,
    )
```

profile of v0, /device:TPU:1, one launch (start us, length us, event | category | flops | bytes accessed | tf_op | source)
XLA Modules:
  0.0 559.6 jit_solution(14840995524542032224)
XLA Ops:
  10.0 3.0 convolution_convert_fusion.1
  13.1 3.7 convolution_convert_fusion
  18.1 5.0 all-to-all-start
  24.6 2.4 fusion.42
  27.1 34.0 %all-gather.5.cloned.1.call-done = bf16[4,1024,256]{2,1,0:T(8,128)(2,1)} async-done(((bf16[1,1024,256]{2,1,0:T(8,128)(2,1)}), bf16[4,1024,256]{2,1,0:T(8,128)(2,1)}) %all-gather.5.cloned.1.call-update) | async-done | bytes 2097168 | tf_op jit(solution)/shard_map/all_gather | solution.py:90
  61.1 36.7 %all-gather.9.cloned.1.call-done = bf16[4096,256]{1,0:T(8,128)(2,1)} async-done(((bf16[1024,256]{1,0:T(8,128)(2,1)}), bf16[4096,256]{1,0:T(8,128)(2,1)}) %all-gather.9.cloned.1.call-update) | async-done | bytes 2097168 | tf_op jit(solution)/shard_map/all_gather | solution.py:89
  97.8 6.6 %convolution_bitcast_fusion = f32[1024,1024]{1,0:T(8,128)} fusion(bf16[4,1024,256]{2,1,0:T(8,128)(2,1)} %bitcast.174, bf16[4,1024,256]{2,1,0:T(8,128)(2,1)} %all-gather.5.cloned.1.call-done), kind=kOutput, calls=%fused_computation.28 | convolution fusion | flops 2147483648 | bytes 8388608 | tf_op jit(solution)/shard_map/jbr,jcr->bc/dot_general | solution.py:101
  104.4 5.3 copy.22
  109.7 9.6 %fusion.3 = f32[1024,1024]{1,0:T(8,128)S(1)} fusion(f32[1024,1024]{0,1:T(8,128)} %copy.22, f32[1024,1024]{1,0:T(8,128)} %convolution_bitcast_fusion, f32[1024]{0:T(1024)S(1)} %bitcast.169, f32[1024]{0:T(1024)S(1)} %bitcast.167), kind=kLoop, calls=%fused_computation.9 | loop fusion | flops 33554432 | bytes 12591104 | tf_op jit(solution)/shard_map/jit(cholesky)/div | solution.py:106
  121.3 11.7 %cholesky.224 = f32[128,128]{1,0:T(8,128)S(1)} custom-call(f32[128,128]{1,0:T(8,128)S(1)} %cholesky.583), custom_call_target="Cholesky" | custom-call | tf_op jit(solution)/shard_map/jit(cholesky)/cholesky | solution.py:106
  133.0 9.8 %custom-call.63 = f32[1,128,128]{1,2,0:T(8,128)S(1)} custom-call(f32[1,128,128]{2,1,0:T(8,128)S(1)} %get-tuple-element.67), custom_call_target="InvertDiagBlocksLowerTriangular" | custom-call | tf_op jit(solution)/shard_map/jit(cholesky)/cholesky | solution.py:106
  142.9 2.5 cholesky.256
  149.3 11.7 %cholesky.245 = f32[128,128]{1,0:T(8,128)S(1)} custom-call(f32[128,128]{1,0:T(8,128)S(1)} %cholesky.587), custom_call_target="Cholesky" | custom-call | tf_op jit(solution)/shard_map/jit(cholesky)/cholesky | solution.py:106
  161.6 10.2 %custom-call.64 = f32[1,128,128]{1,2,0:T(8,128)S(1)} custom-call(f32[1,128,128]{2,1,0:T(8,128)S(1)} %get-tuple-element.64), custom_call_target="InvertDiagBlocksLowerTriangular" | custom-call | tf_op jit(solution)/shard_map/jit(cholesky)/cholesky | solution.py:106
  175.2 11.7 %cholesky.470 = f32[128,128]{1,0:T(8,128)S(1)} custom-call(f32[128,128]{1,0:T(8,128)S(1)} %cholesky.592), custom_call_target="Cholesky" | custom-call | tf_op jit(solution)/shard_map/jit(cholesky)/cholesky | solution.py:106
  188.3 9.8 %custom-call.65 = f32[1,128,128]{1,2,0:T(8,128)S(1)} custom-call(f32[1,128,128]{2,1,0:T(8,128)S(1)} %get-tuple-element.61), custom_call_target="InvertDiagBlocksLowerTriangular" | custom-call | tf_op jit(solution)/shard_map/jit(cholesky)/cholesky | solution.py:106
  201.6 11.9 %cholesky.489 = f32[128,128]{1,0:T(8,128)S(1)} custom-call(f32[128,128]{1,0:T(8,128)S(1)} %cholesky.597), custom_call_target="Cholesky" | custom-call | tf_op jit(solution)/shard_map/jit(cholesky)/cholesky | solution.py:106
  214.8 9.8 %custom-call.66 = f32[1,128,128]{1,2,0:T(8,128)S(1)} custom-call(f32[1,128,128]{2,1,0:T(8,128)S(1)} %get-tuple-element.58), custom_call_target="InvertDiagBlocksLowerTriangular" | custom-call | tf_op jit(solution)/shard_map/jit(cholesky)/cholesky | solution.py:106
  228.1 11.7 %cholesky.508 = f32[128,128]{1,0:T(8,128)S(1)} custom-call(f32[128,128]{1,0:T(8,128)S(1)} %cholesky.602), custom_call_target="Cholesky" | custom-call | tf_op jit(solution)/shard_map/jit(cholesky)/cholesky | solution.py:106
  241.1 9.8 %custom-call.67 = f32[1,128,128]{1,2,0:T(8,128)S(1)} custom-call(f32[1,128,128]{2,1,0:T(8,128)S(1)} %get-tuple-element.55), custom_call_target="InvertDiagBlocksLowerTriangular" | custom-call | tf_op jit(solution)/shard_map/jit(cholesky)/cholesky | solution.py:106
  251.9 2.5 convolution_subtract_fusion.9
  254.4 11.7 %cholesky.528 = f32[128,128]{1,0:T(8,128)S(1)} custom-call(f32[128,128]{1,0:T(8,128)S(1)} %cholesky.607), custom_call_target="Cholesky" | custom-call | tf_op jit(solution)/shard_map/jit(cholesky)/cholesky | solution.py:106
  267.5 9.8 %custom-call.68 = f32[1,128,128]{1,2,0:T(8,128)S(1)} custom-call(f32[1,128,128]{2,1,0:T(8,128)S(1)} %get-tuple-element.52), custom_call_target="InvertDiagBlocksLowerTriangular" | custom-call | tf_op jit(solution)/shard_map/jit(cholesky)/cholesky | solution.py:106
  280.3 11.7 %cholesky.548 = f32[128,128]{1,0:T(8,128)S(1)} custom-call(f32[128,128]{1,0:T(8,128)S(1)} %cholesky.612), custom_call_target="Cholesky" | custom-call | tf_op jit(solution)/shard_map/jit(cholesky)/cholesky | solution.py:106
  293.3 10.2 %custom-call.69 = f32[1,128,128]{1,2,0:T(8,128)S(1)} custom-call(f32[1,128,128]{2,1,0:T(8,128)S(1)} %get-tuple-element.49), custom_call_target="InvertDiagBlocksLowerTriangular" | custom-call | tf_op jit(solution)/shard_map/jit(cholesky)/cholesky | solution.py:106
  306.2 11.7 %cholesky.566 = f32[128,128]{1,0:T(8,128)S(1)} custom-call(f32[128,128]{1,0:T(8,128)S(1)} %convolution_subtract_fusion.11), custom_call_target="Cholesky" | custom-call | tf_op jit(solution)/shard_map/jit(cholesky)/cholesky | solution.py:106
  324.9 4.8 select_select_fusion
  329.7 27.4 %while.1 = (s32[]{:T(128)}, f32[1024,1024]{1,0:T(8,128)}, s32[8,2]{0,1:T(2,128)S(1)}, f32[8,128,128]{2,1,0:T(8,128)}, s32[]{:T(128)}) while((s32[]{:T(128)}, f32[1024,1024]{1,0:T(8,128)}, s32[8,2]{0,1:T(2,128)S(1)}, f32[8,128,128]{2,1,0:T(8,128)}, s32[]{:T(128)}) %tuple.66), condition=%wide.while_cond, body=%wide.while_body.sunk | while | flops 2 | bytes 132705 | solution.py:107
  330.3 2.8 bitcast_dynamic-update-slice_fusion.2
  333.8 2.8 bitcast_dynamic-update-slice_fusion.2
  337.2 2.9 bitcast_dynamic-update-slice_fusion.2
  340.6 2.8 bitcast_dynamic-update-slice_fusion.2
  344.1 2.8 bitcast_dynamic-update-slice_fusion.2
  347.5 2.8 bitcast_dynamic-update-slice_fusion.2
  350.9 2.8 bitcast_dynamic-update-slice_fusion.2
  354.4 2.8 bitcast_dynamic-update-slice_fusion.2
  357.1 79.6 %custom-call.70 = f32[8,128,128]{1,2,0:T(8,128)S(1)} custom-call(f32[8,128,128]{2,1,0:T(8,128)} %get-tuple-element.10), custom_call_target="InvertDiagBlocksLowerTriangular" | custom-call | tf_op jit(solution)/shard_map/jit(_solve_triangular)/triangular_solve | solution.py:107
  452.8 2.6 convolution_subtract_fusion.2
  457.0 2.8 convolution_subtract_fusion.1
  461.2 3.5 convolution_subtract_fusion.3
  466.2 3.4 fusion.27
  469.6 16.3 %fusion.29 = bf16[3,256,1024]{2,1,0:T(8,128)(2,1)S(1)} fusion(f32[1024,1024]{1,0:T(8,128)} %convolution_dynamic-update-slice_fusion, f32[3,256,1024,1]{2,1,0,3:T(8,128)S(1)} %fusion.27, f32[1024]{0:T(1024)S(1)} %bitcast.170, f32[3,256]{1,0:T(4,128)S(1)} %get-tuple-element.84, f32[1024]{0:T(1024)S(1)} %bitcast.168, f32[3,256]{1,0:T(4,128)S(1)} %get-tuple-element.85, ...), kind=kOutput, calls=%fused_computation.40 | convolution fusion | flops 9674686464 | bytes 8927244 | tf_op jit(solution)/shard_map/snb,cb->snc/dot_general | solution.py:113
  489.4 11.0 %all-to-all-start.1 = ((bf16[3,4,64,1024]{3,1,0,2:T(4,128)(2,1)}), bf16[3,4,64,1024]{3,1,0,2:T(4,128)(2,1)}, u32[]{:S(2)}, u32[]{:S(2)}) async-start(bf16[3,4,64,1024]{3,1,0,2:T(4,128)(2,1)} %copy.24), calls=%async_computation.1 | async-start | bytes 3145728 | tf_op jit(solution)/shard_map/all_to_all | solution.py:120
  500.7 6.5 %fusion.142 = (bf16[1024,128]{1,0:T(8,128)(2,1)}, f32[1024,128]{1,0:T(8,128)}) fusion(f32[1024,1024]{1,0:T(8,128)} %convolution_dynamic-update-slice_fusion, f32[1024,128]{1,0:T(8,128)S(1)} %copy-done), kind=kOutput, calls=%fused_computation.240 | convolution fusion | flops 1610743808 | bytes 5505024 | tf_op jit(solution)/shard_map/dot_general | solution.py:116
  509.0 31.1 %all-to-all-done.1 = bf16[3,4,64,1024]{3,1,0,2:T(4,128)(2,1)} async-done(((bf16[3,4,64,1024]{3,1,0,2:T(4,128)(2,1)}), bf16[3,4,64,1024]{3,1,0,2:T(4,128)(2,1)}, u32[]{:S(2)}, u32[]{:S(2)}) %all-to-all-start.1) | async-done | bytes 1572896 | tf_op jit(solution)/shard_map/all_to_all | solution.py:120
  541.9 2.8 gather_fusion
  544.7 3.4 fusion.52
  548.1 2.5 reshape.321
  (120 shorter events, 71.7 us)
Async XLA Ops:
  7.2 493.5 %copy-start = (f32[1024,128]{1,0:T(8,128)S(1)}, f32[1024,128]{1,0:T(8,128)}, u32[]{:S(2)}) copy-start(f32[1024,128]{1,0:T(8,128)} %param.20) | copy-start | bytes 1572868
  7.2 5.9 %copy-start.9 = (bf16[1,1024,256]{2,1,0:T(8,128)(2,1)S(1)}, bf16[1,1024,256]{2,1,0:T(8,128)(2,1)}, u32[]{:S(2)}) copy-start(bf16[1,1024,256]{2,1,0:T(8,128)(2,1)} %param.17) | copy-start | bytes 1572868
  7.2 5.8 %copy-start.8 = (s32[1,3,1]{1,2,0:T(1,128)S(1)}, s32[1,3,1]{1,2,0:T(1,128)}, u32[]{:S(2)}) copy-start(s32[1,3,1]{1,2,0:T(1,128)} %param.12) | copy-start | bytes 40
  7.2 53.9 %all-gather.5.cloned.1.call-start = ((), (), s32[]{:S(2)}) async-start(), calls=%async_computation.2 | async-start | bytes 2621440 | tf_op jit(solution)/shard_map/all_gather | solution.py:90
  9.9 87.9 %all-gather.9.cloned.1.call-start = ((), (), s32[]{:S(2)}) async-start(), calls=%async_computation.4 | async-start | bytes 2621440 | tf_op jit(solution)/shard_map/all_gather | solution.py:89
  16.8 6.3 %copy-start.6 = (s32[2,1024]{1,0:T(2,128)S(1)}, s32[2,1024]{1,0:T(2,128)}, u32[]{:S(2)}) copy-start(s32[2,1024]{1,0:T(2,128)} %param.19) | copy-start | bytes 24580
  16.8 6.3 %copy-start.7 = (s32[3,2,256]{2,1,0:T(2,128)S(1)}, s32[3,2,256]{2,1,0:T(2,128)}, u32[]{:S(2)}) copy-start(s32[3,2,256]{2,1,0:T(2,128)} %param.18) | copy-start | bytes 18436
  16.8 6.3 %copy-start.5 = (s32[64,3]{0,1:T(4,128)S(1)}, s32[64,3]{0,1:T(4,128)}, u32[]{:S(2)}) copy-start(s32[64,3]{0,1:T(4,128)} %param.11) | copy-start | bytes 2308
  18.1 448.1 %all-to-all-start = ((bf16[3,4,256,256]{3,2,0,1:T(8,128)(2,1)}), bf16[3,4,256,256]{3,2,0,1:T(8,128)(2,1)S(1)}, u32[]{:S(2)}, u32[]{:S(2)}) async-start(bf16[3,4,256,256]{3,2,0,1:T(8,128)(2,1)} %copy.20), calls=%async_computation | async-start | bytes 3145728 | tf_op jit(solution)/shard_map/all_to_all | solution.py:95
  119.3 2.0 copy-start.2
  436.7 5.6 %copy-start.1 = (f32[1024,1024]{1,0:T(8,128)S(1)}, f32[1024,1024]{1,0:T(8,128)}, u32[]{:S(2)}) copy-start(f32[1024,1024]{1,0:T(8,128)} %fusion.42) | copy-start | bytes 12582916
  485.9 1.1 copy-start.3
  489.4 50.7 %all-to-all-start.1 = ((bf16[3,4,64,1024]{3,1,0,2:T(4,128)(2,1)}), bf16[3,4,64,1024]{3,1,0,2:T(4,128)(2,1)}, u32[]{:S(2)}, u32[]{:S(2)}) async-start(bf16[3,4,64,1024]{3,1,0,2:T(4,128)(2,1)} %copy.24), calls=%async_computation.1 | async-start | bytes 3145728 | tf_op jit(solution)/shard_map/all_to_all | solution.py:120
  500.4 44.4 %all-gather.7.cloned.1.call-start = ((), (), s32[]{:S(2)}) async-start(), calls=%async_computation.3 | async-start | bytes 1310720 | tf_op jit(solution)/shard_map/all_gather | solution.py:39
  544.7 5.9 %copy-start.4 = (f32[128,1,4,1,512]{4,3,2,1,0:T(1,128)S(1)}, f32[128,1,4,1,512]{4,3,2,1,0:T(1,128)}, u32[]{:S(2)}) copy-start(f32[128,1,4,1,512]{4,3,2,1,0:T(1,128)} %param.21) | copy-start | bytes 3145732
Sparse Core Ops, SparseCore 0:
  10.0 51.0 all-gather.4
  63.5 34.2 all-gather.8
  507.3 26.3 all-gather.6
where the time goes:
time: 567 us; the launch traced here: 560 us
  other arithmetic  275 us (49%)
  waiting for transfers between devices  102 us (18%)
  matrix products  95.5 us (17%)
  local copies, waits for them, and re-layouts  50.8 us (9%)
  between operations  20.4 us (4%)
  starting transfers between devices  16.4 us (3%)
    another operation x30, other arithmetic, per_device(): factor = jnp.linalg.cholesky(diag_system)  172 us
    another operation x3, other arithmetic, per_device(): inverse = jax.scipy.linalg.solve_triangular(factor, identity, lower=True)  84.4 us
    all_gather x1, waiting for transfers between devices, per_device(): lax.all_gather(diag_low[None], 'cols', axis=0, tiled=True)  36.7 us
    all_gather x1, waiting for transfers between devices, per_device(): lax.all_gather(diagonal_left_factor[None], 'cols', axis=0, tiled=True)  34 us
    all_to_all x1, waiting for transfers between devices, per_device(): lax.all_to_all(outgoing_rows, 'rows', split_axis=2, concat_axis=2, tiled=...  31.1 us
    another operation x15, matrix products, per_device(): inverse = jax.scipy.linalg.solve_triangular(factor, identity, lower=True)  29.4 us
    another operation x24, local copies, waits for them, and re-layouts  27.4 us
    another operation x14, matrix products, per_device(): factor = jnp.linalg.cholesky(diag_system)  23.3 us
  transfers between devices with their start and end apart: 5, of which 3 were waited for; matrix products, arithmetic and copies ran while one was open for 69% of the time, Pallas kernels for 0%

commit v1 on v0

--- a/solution.py
+++ b/solution.py
@@ -6,6 +6,27 @@
 GX = 1024
 length_scale = 0.3
 nugget = 1.0
+
+
+def collect(shard, axis, dim):
+    size, place, rows = (lax.axis_size(axis), lax.axis_index(axis), shard.shape[dim])
+    forward = [(i, (i + 1) % size) for i in range(size)]
+    left = [(i, (i - 1) % size) for i in range(size)]
+    out = jnp.zeros((*shard.shape[:dim], size * rows, *shard.shape[dim + 1 :]), shard.dtype)
+    out = lax.dynamic_update_slice_in_dim(out, shard, place * rows, axis=dim)
+    from_left = from_right = shard
+    middle = size // 2
+    for step in range(1, middle + 1):
+        from_left = lax.ppermute(from_left, axis, forward)
+        out = lax.dynamic_update_slice_in_dim(
+            out, from_left, (place - step) % size * rows, axis=dim
+        )
+        if step < size - middle:
+            from_right = lax.ppermute(from_right, axis, left)
+            out = lax.dynamic_update_slice_in_dim(
+                out, from_right, (place + step) % size * rows, axis=dim
+            )
+    return out
 
 
 def matern(first_x, first_y, second_x, second_y):
@@ -86,7 +107,7 @@
         jnp.bfloat16
     )
     gathered_low, gathered_left = (
-        lax.all_gather(diag_low[None], "cols", axis=0, tiled=True),
+        collect(diag_low[None], "cols", 0),
         lax.all_gather(diagonal_left_factor[None], "cols", axis=0, tiled=True),
     )
     outgoing_low = low_rows.reshape(slot_count, col_devices, quarter, rank_max)

time: 567 us -> 547 us (0.965)
  waiting for transfers between devices: 102 us -> 69.9 us
    ppermute x0 -> x3, waiting for transfers between devices: none -> 38.8 us  [the longest x2 38.8 us: collect(): from_left = lax.ppermute(from_left, axis, forward)]
    all_gather x1 -> x0, waiting for transfers between devices: 36.7 us -> none  [per_device(): lax.all_gather(diag_low[None], 'cols', axis=0, tiled=True)]
    all_gather x1, waiting for transfers between devices: 34 us -> 0.02 us  [per_device(): lax.all_gather(diagonal_left_factor[None], 'cols', axis=0, tiled=True)]
  transfers between devices with their start and end apart: 5 -> 7, of which waited for: 3 -> 2; matrix products, arithmetic and copies ran while one was open for 69% -> 73% of each run, Pallas kernels for 0% -> 0%
where the time goes in v1:
time: 547 us; the launch traced here: 538 us
  other arithmetic  275 us (50%)
  matrix products  96 us (18%)
  waiting for transfers between devices  69.9 us (13%)
  local copies, waits for them, and re-layouts  54.7 us (10%)
  starting transfers between devices  22 us (4%)
  between operations  20.7 us (4%)
    another operation x30, other arithmetic, per_device(): factor = jnp.linalg.cholesky(diag_system)  173 us
    another operation x3, other arithmetic, per_device(): inverse = jax.scipy.linalg.solve_triangular(factor, identity, lower=True)  84.4 us
    ppermute x2, waiting for transfers between devices, collect(): from_left = lax.ppermute(from_left, axis, forward)  38.8 us
    all_to_all x1, waiting for transfers between devices, per_device(): lax.all_to_all(outgoing_rows, 'rows', split_axis=2, concat_axis=2, tiled=...  31.1 us
    another operation x15, matrix products, per_device(): inverse = jax.scipy.linalg.solve_triangular(factor, identity, lower=True)  29.4 us
    another operation x24, local copies, waits for them, and re-layouts  27.5 us
    another operation x14, matrix products, per_device(): factor = jnp.linalg.cholesky(diag_system)  23.3 us
    dot_general x1, matrix products, per_device(): jnp.einsum('snb,cb->snc', system_rows, inverse, precision=lax.Precision.H...  16.3 us
  transfers between devices with their start and end apart: 7, of which 2 were waited for; matrix products, arithmetic and copies ran while one was open for 73% of the time, Pallas kernels for 0%

profile of v1, /device:TPU:1, one launch (start us, length us, event | category | flops | bytes accessed | tf_op | source)
XLA Modules:
  0.0 537.9 jit_solution(17912168035515724245)
XLA Ops:
  10.0 3.1 constant_dynamic-update-slice_fusion.29
  16.7 5.0 convolution_convert_fusion
  21.7 2.7 copy.20
  24.3 4.5 all-to-all-start
  28.9 2.4 fusion.42
  35.4 38.8 %collective-permute-done.2 = bf16[1,1024,256]{2,1,0:T(8,128)(2,1)} collective-permute-done((bf16[1,1024,256]{2,1,0:T(8,128)(2,1)S(1)}, bf16[1,1024,256]{2,1,0:T(8,128)(2,1)}, u32[]{:S(2)}, u32[]{:S(2)}) %collective-permute-start.2) | collective-permute-done | bytes 524320 | tf_op jit(solution)/shard_map/ppermute | solution.py:20
  75.3 5.9 %convolution_bitcast_fusion = f32[1024,1024]{1,0:T(8,128)} fusion(bf16[4,1024,256]{2,1,0:T(8,128)(2,1)S(1)} %constant_dynamic-update-slice_fusion.26, bf16[4,1024,256]{2,1,0:T(8,128)(2,1)} %all-gather.3.cloned.1.call-done), kind=kOutput, calls=%fused_computation.28 | convolution fusion | flops 2147483648 | bytes 8388608 | tf_op jit(solution)/shard_map/jbr,jcr->bc/dot_general | solution.py:122
  81.2 5.3 copy.22
  86.5 9.6 %fusion.3 = f32[1024,1024]{1,0:T(8,128)S(1)} fusion(f32[1024,1024]{0,1:T(8,128)} %copy.22, f32[1024,1024]{1,0:T(8,128)} %convolution_bitcast_fusion, f32[1024]{0:T(1024)S(1)} %bitcast.174, f32[1024]{0:T(1024)S(1)} %bitcast.172), kind=kLoop, calls=%fused_computation.9 | loop fusion | flops 33554432 | bytes 12591104 | tf_op jit(solution)/shard_map/jit(cholesky)/div | solution.py:127
  98.1 11.7 %cholesky.224 = f32[128,128]{1,0:T(8,128)S(1)} custom-call(f32[128,128]{1,0:T(8,128)S(1)} %cholesky.583), custom_call_target="Cholesky" | custom-call | tf_op jit(solution)/shard_map/jit(cholesky)/cholesky | solution.py:127
  109.9 2.5 cholesky.256
  112.4 9.8 %custom-call.63 = f32[1,128,128]{1,2,0:T(8,128)S(1)} custom-call(f32[1,128,128]{2,1,0:T(8,128)S(1)} %get-tuple-element.67), custom_call_target="InvertDiagBlocksLowerTriangular" | custom-call | tf_op jit(solution)/shard_map/jit(cholesky)/cholesky | solution.py:127
  126.1 11.7 %cholesky.245 = f32[128,128]{1,0:T(8,128)S(1)} custom-call(f32[128,128]{1,0:T(8,128)S(1)} %cholesky.587), custom_call_target="Cholesky" | custom-call | tf_op jit(solution)/shard_map/jit(cholesky)/cholesky | solution.py:127
  138.5 10.2 %custom-call.64 = f32[1,128,128]{1,2,0:T(8,128)S(1)} custom-call(f32[1,128,128]{2,1,0:T(8,128)S(1)} %get-tuple-element.64), custom_call_target="InvertDiagBlocksLowerTriangular" | custom-call | tf_op jit(solution)/shard_map/jit(cholesky)/cholesky | solution.py:127
  152.0 11.7 %cholesky.470 = f32[128,128]{1,0:T(8,128)S(1)} custom-call(f32[128,128]{1,0:T(8,128)S(1)} %cholesky.592), custom_call_target="Cholesky" | custom-call | tf_op jit(solution)/shard_map/jit(cholesky)/cholesky | solution.py:127
  165.1 9.8 %custom-call.65 = f32[1,128,128]{1,2,0:T(8,128)S(1)} custom-call(f32[1,128,128]{2,1,0:T(8,128)S(1)} %get-tuple-element.61), custom_call_target="InvertDiagBlocksLowerTriangular" | custom-call | tf_op jit(solution)/shard_map/jit(cholesky)/cholesky | solution.py:127
  178.4 11.9 %cholesky.489 = f32[128,128]{1,0:T(8,128)S(1)} custom-call(f32[128,128]{1,0:T(8,128)S(1)} %cholesky.597), custom_call_target="Cholesky" | custom-call | tf_op jit(solution)/shard_map/jit(cholesky)/cholesky | solution.py:127
  191.6 9.8 %custom-call.66 = f32[1,128,128]{1,2,0:T(8,128)S(1)} custom-call(f32[1,128,128]{2,1,0:T(8,128)S(1)} %get-tuple-element.58), custom_call_target="InvertDiagBlocksLowerTriangular" | custom-call | tf_op jit(solution)/shard_map/jit(cholesky)/cholesky | solution.py:127
  204.9 11.7 %cholesky.508 = f32[128,128]{1,0:T(8,128)S(1)} custom-call(f32[128,128]{1,0:T(8,128)S(1)} %cholesky.602), custom_call_target="Cholesky" | custom-call | tf_op jit(solution)/shard_map/jit(cholesky)/cholesky | solution.py:127
  218.0 9.8 %custom-call.67 = f32[1,128,128]{1,2,0:T(8,128)S(1)} custom-call(f32[1,128,128]{2,1,0:T(8,128)S(1)} %get-tuple-element.55), custom_call_target="InvertDiagBlocksLowerTriangular" | custom-call | tf_op jit(solution)/shard_map/jit(cholesky)/cholesky | solution.py:127
  228.8 2.5 slice_subtract_fusion.4
  231.3 11.7 %cholesky.528 = f32[128,128]{1,0:T(8,128)S(1)} custom-call(f32[128,128]{1,0:T(8,128)S(1)} %cholesky.607), custom_call_target="Cholesky" | custom-call | tf_op jit(solution)/shard_map/jit(cholesky)/cholesky | solution.py:127
  244.4 9.8 %custom-call.68 = f32[1,128,128]{1,2,0:T(8,128)S(1)} custom-call(f32[1,128,128]{2,1,0:T(8,128)S(1)} %get-tuple-element.52), custom_call_target="InvertDiagBlocksLowerTriangular" | custom-call | tf_op jit(solution)/shard_map/jit(cholesky)/cholesky | solution.py:127
  257.2 11.7 %cholesky.548 = f32[128,128]{1,0:T(8,128)S(1)} custom-call(f32[128,128]{1,0:T(8,128)S(1)} %cholesky.612), custom_call_target="Cholesky" | custom-call | tf_op jit(solution)/shard_map/jit(cholesky)/cholesky | solution.py:127
  270.2 10.2 %custom-call.69 = f32[1,128,128]{1,2,0:T(8,128)S(1)} custom-call(f32[1,128,128]{2,1,0:T(8,128)S(1)} %get-tuple-element.49), custom_call_target="InvertDiagBlocksLowerTriangular" | custom-call | tf_op jit(solution)/shard_map/jit(cholesky)/cholesky | solution.py:127
  283.0 11.7 %cholesky.566 = f32[128,128]{1,0:T(8,128)S(1)} custom-call(f32[128,128]{1,0:T(8,128)S(1)} %slice_subtract_fusion.6), custom_call_target="Cholesky" | custom-call | tf_op jit(solution)/shard_map/jit(cholesky)/cholesky | solution.py:127
  301.7 4.8 select_select_fusion
  306.6 27.5 %while.1 = (s32[]{:T(128)}, f32[1024,1024]{1,0:T(8,128)}, s32[8,2]{0,1:T(2,128)S(1)}, f32[8,128,128]{2,1,0:T(8,128)}, s32[]{:T(128)}) while((s32[]{:T(128)}, f32[1024,1024]{1,0:T(8,128)}, s32[8,2]{0,1:T(2,128)S(1)}, f32[8,128,128]{2,1,0:T(8,128)}, s32[]{:T(128)}) %tuple.67), condition=%wide.while_cond, body=%wide.while_body.sunk | while | flops 2 | bytes 132705 | solution.py:128
  307.2 2.8 bitcast_dynamic-update-slice_fusion.2
  310.6 2.8 bitcast_dynamic-update-slice_fusion.2
  314.1 2.8 bitcast_dynamic-update-slice_fusion.2
  317.5 2.8 bitcast_dynamic-update-slice_fusion.2
  320.9 2.8 bitcast_dynamic-update-slice_fusion.2
  324.4 2.8 bitcast_dynamic-update-slice_fusion.2
  327.8 2.8 bitcast_dynamic-update-slice_fusion.2
  331.3 2.8 bitcast_dynamic-update-slice_fusion.2
  334.1 79.6 %custom-call.70 = f32[8,128,128]{1,2,0:T(8,128)S(1)} custom-call(f32[8,128,128]{2,1,0:T(8,128)} %get-tuple-element.10), custom_call_target="InvertDiagBlocksLowerTriangular" | custom-call | tf_op jit(solution)/shard_map/jit(_solve_triangular)/triangular_solve | solution.py:128
  429.8 2.6 convolution_subtract_fusion.2
  433.9 2.8 convolution_subtract_fusion.1
  438.2 3.5 convolution_subtract_fusion.3
  443.1 3.2 fusion.27
  446.3 16.3 %fusion.29 = bf16[3,256,1024]{2,1,0:T(8,128)(2,1)S(1)} fusion(f32[1024,1024]{1,0:T(8,128)} %convolution_dynamic-update-slice_fusion, f32[3,256,1024,1]{2,1,0,3:T(8,128)S(1)} %fusion.27, f32[1024]{0:T(1024)S(1)} %bitcast.175, f32[3,256]{1,0:T(4,128)S(1)} %get-tuple-element.86, f32[1024]{0:T(1024)S(1)} %bitcast.173, f32[3,256]{1,0:T(4,128)S(1)} %get-tuple-element.87, ...), kind=kOutput, calls=%fused_computation.40 | convolution fusion | flops 9674686464 | bytes 8927244 | tf_op jit(solution)/shard_map/snb,cb->snc/dot_general | solution.py:134
  466.1 12.2 %all-to-all-start.1 = ((bf16[3,4,64,1024]{3,1,0,2:T(4,128)(2,1)}), bf16[3,4,64,1024]{3,1,0,2:T(4,128)(2,1)}, u32[]{:S(2)}, u32[]{:S(2)}) async-start(bf16[3,4,64,1024]{3,1,0,2:T(4,128)(2,1)} %copy.24), calls=%async_computation.1 | async-start | bytes 3145728 | tf_op jit(solution)/shard_map/all_to_all | solution.py:141
  478.7 6.5 %fusion.162 = (bf16[1024,128]{1,0:T(8,128)(2,1)}, f32[1024,128]{1,0:T(8,128)}) fusion(f32[1024,1024]{1,0:T(8,128)} %convolution_dynamic-update-slice_fusion, f32[1024,128]{1,0:T(8,128)S(1)} %copy-done), kind=kOutput, calls=%fused_computation.252 | convolution fusion | flops 1610743808 | bytes 5505024 | tf_op jit(solution)/shard_map/dot_general | solution.py:137
  487.0 31.1 %all-to-all-done.1 = bf16[3,4,64,1024]{3,1,0,2:T(4,128)(2,1)} async-done(((bf16[3,4,64,1024]{3,1,0,2:T(4,128)(2,1)}), bf16[3,4,64,1024]{3,1,0,2:T(4,128)(2,1)}, u32[]{:S(2)}, u32[]{:S(2)}) %all-to-all-start.1) | async-done | bytes 1572896 | tf_op jit(solution)/shard_map/all_to_all | solution.py:141
  519.9 2.8 gather_fusion
  522.7 3.4 fusion.52
  526.1 2.5 reshape.320
  (127 shorter events, 77.7 us)
Async XLA Ops:
  7.2 471.5 %copy-start = (f32[1024,128]{1,0:T(8,128)S(1)}, f32[1024,128]{1,0:T(8,128)}, u32[]{:S(2)}) copy-start(f32[1024,128]{1,0:T(8,128)} %param.20) | copy-start | bytes 1572868
  7.2 9.4 %copy-start.8 = (s32[1,3,1]{1,2,0:T(1,128)S(1)}, s32[1,3,1]{1,2,0:T(1,128)}, u32[]{:S(2)}) copy-start(s32[1,3,1]{1,2,0:T(1,128)} %param.12) | copy-start | bytes 40
  7.2 68.1 %all-gather.3.cloned.1.call-start = ((), (), s32[]{:S(2)}) async-start(), calls=%async_computation.2 | async-start | bytes 2621440 | tf_op jit(solution)/shard_map/all_gather | solution.py:111
  13.0 19.6 %collective-permute-start = (bf16[1,1024,256]{2,1,0:T(8,128)(2,1)}, bf16[1,1024,256]{2,1,0:T(8,128)(2,1)S(1)}, u32[]{:S(2)}, u32[]{:S(2)}) collective-permute-start(bf16[1,1024,256]{2,1,0:T(8,128)(2,1)} %get-tuple-element.75), channel_id=1, source_target_pairs={{0,1},{1,2},{2,3},{3,0},{4,5},{5,6},{6,7},{7,4},{8,9},{9,10},{10,1... | collective-permute-start | bytes 1572872 | tf_op jit(solution)/shard_map/ppermute | solution.py:20
  15.2 19.1 %collective-permute-start.1 = (bf16[1,1024,256]{2,1,0:T(8,128)(2,1)}, bf16[1,1024,256]{2,1,0:T(8,128)(2,1)}, u32[]{:S(2)}, u32[]{:S(2)}) collective-permute-start(bf16[1,1024,256]{2,1,0:T(8,128)(2,1)} %get-tuple-element.75), channel_id=1, source_target_pairs={{0,3},{1,0},{2,1},{3,2},{4,7},{5,4},{6,5},{7,6},{8,11},{9,8},{10,9... | collective-permute-start | bytes 1572872 | tf_op jit(solution)/shard_map/ppermute | solution.py:25
  21.7 7.2 %copy-start.7 = (s32[3,2,256]{2,1,0:T(2,128)S(1)}, s32[3,2,256]{2,1,0:T(2,128)}, u32[]{:S(2)}) copy-start(s32[3,2,256]{2,1,0:T(2,128)} %param.18) | copy-start | bytes 18436
  24.3 7.0 %copy-start.6 = (s32[2,1024]{1,0:T(2,128)S(1)}, s32[2,1024]{1,0:T(2,128)}, u32[]{:S(2)}) copy-start(s32[2,1024]{1,0:T(2,128)} %param.19) | copy-start | bytes 24580
  24.3 9.7 %copy-start.5 = (s32[64,3]{0,1:T(4,128)S(1)}, s32[64,3]{0,1:T(4,128)}, u32[]{:S(2)}) copy-start(s32[64,3]{0,1:T(4,128)} %param.11) | copy-start | bytes 2308
  24.3 418.7 %all-to-all-start = ((bf16[3,4,256,256]{3,2,0,1:T(8,128)(2,1)}), bf16[3,4,256,256]{3,2,0,1:T(8,128)(2,1)}, u32[]{:S(2)}, u32[]{:S(2)}) async-start(bf16[3,4,256,256]{3,2,0,1:T(8,128)(2,1)} %copy.20), calls=%async_computation | async-start | bytes 3145728 | tf_op jit(solution)/shard_map/all_to_all | solution.py:116
  32.6 41.5 %collective-permute-start.2 = (bf16[1,1024,256]{2,1,0:T(8,128)(2,1)S(1)}, bf16[1,1024,256]{2,1,0:T(8,128)(2,1)}, u32[]{:S(2)}, u32[]{:S(2)}) collective-permute-start(bf16[1,1024,256]{2,1,0:T(8,128)(2,1)S(1)} %collective-permute-done), channel_id=1, source_target_pairs={{0,1},{1,2},{2,3},{3,0},{4,5},{5,6},{6,7},{7,4},{8,9},{9,10},{10,1... | collective-permute-start | bytes 1572872 | tf_op jit(solution)/shard_map/ppermute | solution.py:20
  96.1 2.0 copy-start.2
  413.6 5.6 %copy-start.1 = (f32[1024,1024]{1,0:T(8,128)S(1)}, f32[1024,1024]{1,0:T(8,128)}, u32[]{:S(2)}) copy-start(f32[1024,1024]{1,0:T(8,128)} %fusion.42) | copy-start | bytes 12582916
  436.7 6.4 %copy-start.9 = (bf16[4,1024,256]{2,1,0:T(8,128)(2,1)S(1)}, bf16[4,1024,256]{2,1,0:T(8,128)(2,1)}, u32[]{:S(2)}) copy-start(bf16[4,1024,256]{2,1,0:T(8,128)(2,1)} %all-gather.3.cloned.1.call-done) | copy-start | bytes 6291460
  462.6 1.1 copy-start.3
  466.1 51.9 %all-to-all-start.1 = ((bf16[3,4,64,1024]{3,1,0,2:T(4,128)(2,1)}), bf16[3,4,64,1024]{3,1,0,2:T(4,128)(2,1)}, u32[]{:S(2)}, u32[]{:S(2)}) async-start(bf16[3,4,64,1024]{3,1,0,2:T(4,128)(2,1)} %copy.24), calls=%async_computation.1 | async-start | bytes 3145728 | tf_op jit(solution)/shard_map/all_to_all | solution.py:141
  478.3 44.4 %all-gather.5.cloned.1.call-start = ((), (), s32[]{:S(2)}) async-start(), calls=%async_computation.3 | async-start | bytes 1310720 | tf_op jit(solution)/shard_map/all_gather | solution.py:60
  522.7 5.9 %copy-start.4 = (f32[128,1,4,1,512]{4,3,2,1,0:T(1,128)S(1)}, f32[128,1,4,1,512]{4,3,2,1,0:T(1,128)}, u32[]{:S(2)}) copy-start(f32[128,1,4,1,512]{4,3,2,1,0:T(1,128)} %param.21) | copy-start | bytes 3145732
Sparse Core Ops, SparseCore 0:
  10.0 57.9 all-gather.2
  485.3 26.5 all-gather.4
